TPU v7x, 32 devices: a whole 2x2x4 slice. The times are simulated.
32 devices in a mesh: gx: 4 (over y, x), gy: 2 (over core), gz: 4 (over z).
Axes of the slice: x: 2, y: 2, z: 4, core: 2. Of those that a mesh axis runs over, the one named last changes fastest.
Arguments:
- correction: float32 [64, 64, 512], P('gz', 'gx', 'gy'), may hold values from -6 to 6
- residual: float32 [64, 64, 512], P('gz', 'gx', 'gy'), may hold values from -4 to 6
- state: float32 [64, 64, 512], P('gz', 'gx', 'gy'), may hold values from -1 to 1
- spacing_level: int32 [64], replicated, may hold values from 0 to 3
- line_colour: int32 [64, 512], P('gx', 'gy'), may hold values from 0 to 1
Outputs:
- smoothed: float32 [64, 64, 512], P('gz', 'gx', 'gy')
All inputs are finite; a program needn't handle non-finite values.
Results may differ from a plain program's by a relative error of at most 0.0003.
Values sent between devices are 32-bit elements; how exact they have to be, the bound alone decides.
A program may use at most 64 MiB of HBM per device.

v0:
```python
import jax
import jax.numpy as jnp
from jax import lax
from jax.sharding import PartitionSpec as P

coef_z = 1000.0
coef_x = 0.3
coef_y = 0.2
bratu_lambda = 0.2


def extended(block, sides, width):
    for axis, dim in sides:
        count = lax.axis_size(axis)
        forward = [(i, i + 1) for i in range(count - 1)]
        backward = [(target, source) for source, target in forward]
        low = lax.ppermute(
            lax.slice_in_dim(block, block.shape[dim] - width, None, axis=dim), axis, forward
        )
        high = lax.ppermute(lax.slice_in_dim(block, 0, width, axis=dim), axis, backward)
        block = jnp.concatenate([low, block, high], axis=dim)
    return block


def face_coupling(spacing_level):
    spacing_cells = 0.8 * jnp.power(1.3, spacing_level.astype(jnp.float32))
    inner_faces = coef_z * 2.0 / (spacing_cells[:-1] + spacing_cells[1:])
    nothing = jnp.zeros((1,), jnp.float32)
    face_low = jnp.concatenate([nothing, inner_faces])
    face_high = jnp.concatenate([inner_faces, nothing])
    return (spacing_cells, face_low, face_high)


def move_rows(values, stride, filler):
    length = values.shape[0]
    padding = jnp.full((abs(stride),) + values.shape[1:], filler, values.dtype)
    if stride > 0:
        return jnp.concatenate([padding, values[: length - stride]], 0)
    return jnp.concatenate([values[-stride:], padding], 0)


def factor_local(below_coef, centre, above_coef):
    length = centre.shape[0]
    sections = []
    stride = 1
    while stride < length:
        before_low = move_rows(below_coef, stride, 0.0)
        before_mid = move_rows(centre, stride, 1.0)
        before_high = move_rows(above_coef, stride, 0.0)
        beyond_low = move_rows(below_coef, -stride, 0.0)
        beyond_mid = move_rows(centre, -stride, 1.0)
        beyond_high = move_rows(above_coef, -stride, 0.0)
        weight_low = -below_coef / before_mid
        weight_high = -above_coef / beyond_mid
        centre = centre + weight_low * before_high + weight_high * beyond_low
        below_coef = weight_low * before_low
        above_coef = weight_high * beyond_high
        sections.append((weight_low, weight_high))
        stride = stride * 2
    return (sections, centre)


def apply_local(source, sections, centre):
    stride = 1
    for weight_low, weight_high in sections:
        source = (
            source
            + weight_low * move_rows(source, stride, 0.0)
            + weight_high * move_rows(source, -stride, 0.0)
        )
        stride = stride * 2
    return source / centre


def on_device(correction, residual, state, spacing_level, line_colour):
    depth = correction.shape[0]
    device_place = lax.axis_index("gz")
    spacing_all, face_low_all, face_high_all = face_coupling(spacing_level)
    offset_rows = device_place * depth
    spacing_cells = lax.dynamic_slice_in_dim(spacing_all, offset_rows, depth)
    face_low = lax.dynamic_slice_in_dim(face_low_all, offset_rows, depth)
    face_high = lax.dynamic_slice_in_dim(face_high_all, offset_rows, depth)
    column = spacing_cells[:, None, None]
    centre = (face_low + face_high)[:, None, None] + column * (
        2.0 * coef_x + 2.0 * coef_y - bratu_lambda * jnp.exp(state)
    )
    line_shape = centre.shape
    row_column = jnp.arange(depth)[:, None, None]
    edge_rows = (row_column == 0) | (row_column == depth - 1)
    low_full = jnp.broadcast_to((-face_low)[:, None, None], line_shape)
    high_full = jnp.broadcast_to((-face_high)[:, None, None], line_shape)
    inner_low = jnp.where((row_column <= 1) | (row_column == depth - 1), 0.0, low_full)
    inner_high = jnp.where((row_column >= depth - 2) | (row_column == 0), 0.0, high_full)
    inner_centre = jnp.where(edge_rows, 1.0, centre)
    sections_local, centre_local = factor_local(inner_low, inner_centre, inner_high)
    from_first = apply_local(
        jnp.where(row_column == 1, -low_full, 0.0), sections_local, centre_local
    )
    from_last = apply_local(
        jnp.where(row_column == depth - 2, -high_full, 0.0), sections_local, centre_local
    )
    first_low = low_full[0]
    first_mid = centre[0] + high_full[0] * from_first[1]
    first_high = high_full[0] * from_last[1]
    last_low = low_full[depth - 1] * from_first[depth - 2]
    last_mid = centre[depth - 1] + low_full[depth - 1] * from_last[depth - 2]
    last_high = high_full[depth - 1]
    coupled = jnp.stack(
        [
            jnp.stack([first_low, last_low], 0),
            jnp.stack([first_mid, last_mid], 0),
            jnp.stack([first_high, last_high], 0),
        ],
        0,
    )
    gathered = lax.all_gather(coupled, "gz", axis=1, tiled=True)
    sections_reduced, centre_reduced = factor_local(gathered[0], gathered[1], gathered[2])
    iterate = correction
    for colour in range(2):
        padded = extended(iterate, (("gx", 1), ("gy", 2)), 1)
        beside = coef_x * (padded[:, 2:, 1:-1] + padded[:, :-2, 1:-1]) + coef_y * (
            padded[:, 1:-1, 2:] + padded[:, 1:-1, :-2]
        )
        source = column * (residual + beside)
        interior = apply_local(jnp.where(edge_rows, 0.0, source), sections_local, centre_local)
        first_source = source[0] - high_full[0] * interior[1]
        last_source = source[depth - 1] - low_full[depth - 1] * interior[depth - 2]
        source_pair = jnp.stack([first_source, last_source], 0)
        all_sources = lax.all_gather(source_pair, "gz", axis=0, tiled=True)
        solution = apply_local(all_sources, sections_reduced, centre_reduced)
        ends_value = lax.dynamic_slice_in_dim(solution, 2 * device_place, 2, 0)
        first_cell = ends_value[0]
        last_cell = ends_value[1]
        inside = interior + from_first * first_cell[None] + from_last * last_cell[None]
        solved = jnp.where(
            row_column == 0,
            first_cell[None],
            jnp.where(row_column == depth - 1, last_cell[None], inside),
        )
        iterate = jnp.where((line_colour == colour)[None], solved, iterate)
    return iterate


def solution(mesh):
    return jax.shard_map(
        on_device,
        mesh=mesh,
        in_specs=(
            P("gz", "gx", "gy"),
            P("gz", "gx", "gy"),
            P("gz", "gx", "gy"),
            P(),
            P("gx", "gy"),
        ),
        out_specs=P("gz", "gx", "gy"),
        check_vma=False,
    )
```

profile of v0, /device:TPU:12, one launch (start us, length us, event | category | flops | bytes accessed | tf_op | source)
XLA Modules:
  0.0 85.7 jit_solution(15522667361424550462)
XLA Ops:
  0.0 1.0 %fusion.55 = (f32[16,1,256]{2,1,0:T(1,128)S(1)}, f32[16,1,256]{2,1,0:T(1,128)S(1)}) fusion(f32[16,16,256]{2,1,0:T(8,128)} %param.5), kind=kLoop, calls=%fused_computation.170 | loop fusion | bytes 65536 | tf_op jit(solution)/shard_map/slice | solution.py:18
  1.0 3.3 %collective-permute-start = (f32[16,1,256]{2,1,0:T(1,128)S(1)}, f32[16,1,256]{2,1,0:T(1,128)S(1)}, u32[]{:S(2)}, u32[]{:S(2)}) collective-permute-start(f32[16,1,256]{2,1,0:T(1,128)S(1)} %get-tuple-element.94), channel_id=1, source_target_pairs={{8,0},{16,8},{24,16},{9,1},{17,9},{25,17},{10,2},{18,10},{26,18},{... | collective-permute-start | bytes 49160 | tf_op jit(solution)/shard_map/ppermute | solution.py:20
  4.3 2.5 %collective-permute-start.1 = (f32[16,1,256]{2,1,0:T(1,128)S(1)}, f32[16,1,256]{2,1,0:T(1,128)S(1)}, u32[]{:S(2)}, u32[]{:S(2)}) collective-permute-start(f32[16,1,256]{2,1,0:T(1,128)S(1)} %get-tuple-element.93), channel_id=1, source_target_pairs={{0,8},{8,16},{16,24},{1,9},{9,17},{17,25},{2,10},{10,18},{18,26},{... | collective-permute-start | bytes 49160 | tf_op jit(solution)/shard_map/ppermute | solution.py:17
  6.9 0.6 copy-done.4
  8.8 0.6 fusion.84
  9.5 1.4 %collective-permute-done.1 = f32[16,1,256]{2,1,0:T(1,128)S(1)} collective-permute-done((f32[16,1,256]{2,1,0:T(1,128)S(1)}, f32[16,1,256]{2,1,0:T(1,128)S(1)}, u32[]{:S(2)}, u32[]{:S(2)}) %collective-permute-start.1) | collective-permute-done | bytes 16416 | tf_op jit(solution)/shard_map/ppermute | solution.py:17
  11.1 1.4 %collective-permute-start.2 = (f32[16,18,1]{2,1,0:T(8,128)S(1)}, f32[16,18,1]{2,1,0:T(8,128)S(1)}, u32[]{:S(2)}, u32[]{:S(2)}) collective-permute-start(f32[16,18,1]{2,1,0:T(8,128)S(1)} %get-tuple-element.63), channel_id=1, source_target_pairs={{4,0},{5,1},{6,2},{7,3},{12,8},{13,9},{14,10},{15,11},{20,16},{21,... | collective-permute-start | bytes 3464 | tf_op jit(solution)/shard_map/ppermute | solution.py:20
  12.5 3.0 %collective-permute-start.3 = (f32[16,18,1]{2,1,0:T(8,128)S(1)}, f32[16,18,1]{2,1,0:T(8,128)S(1)}, u32[]{:S(2)}, u32[]{:S(2)}) collective-permute-start(f32[16,18,1]{2,1,0:T(8,128)S(1)} %get-tuple-element.64), channel_id=1, source_target_pairs={{0,4},{1,5},{2,6},{3,7},{8,12},{9,13},{10,14},{11,15},{16,20},{17,... | collective-permute-start | bytes 3464 | tf_op jit(solution)/shard_map/ppermute | solution.py:17
  15.7 0.9 %collective-permute-done.3 = f32[16,18,1]{2,1,0:T(8,128)S(1)} collective-permute-done((f32[16,18,1]{2,1,0:T(8,128)S(1)}, f32[16,18,1]{2,1,0:T(8,128)S(1)}, u32[]{:S(2)}, u32[]{:S(2)}) %collective-permute-start.3) | collective-permute-done | bytes 1184 | tf_op jit(solution)/shard_map/ppermute | solution.py:17
  19.8 1.2 %slice_multiply_fusion.5 = (f32[1,16,256]{2,1,0:T(8,128)S(1)}, f32[1,16,256]{2,1,0:T(8,128)S(1)}, f32[1,16,256]{2,1,0:T(8,128)S(1)}, f32[1,16,256]{2,1,0:T(8,128)S(1)}) fusion(f32[16,16,256]{2,1,0:T(8,128)S(1)} %get-tuple-element.36, f32[]{:T(128)} %bitcast.1, f32[]{:T(128)} %bitcast, f32[16,16,256]{2,1,0:T(8,128)S(1)} %get-tuple-element.158, ...), kind=kLoop, calls=%fused_computation.138 | loop fusion | flops 24576 | bytes 163848 | tf_op jit(solution)/shard_map/mul | solution.py:105
  21.1 0.7 pad_bitcast_fusion.1
  21.7 0.6 pad_bitcast_fusion
  22.4 15.6 %all_gather.10 = f32[3,8,16,256]{3,2,1,0:T(8,128)S(1)} all-gather(f32[3,2,16,256]{3,2,1,0:T(8,128)S(1)} %pad_maximum_fusion.18), channel_id=1, replica_groups=mesh['gx'=4,'gy'=2,'gz'=4] {'gz'}, dimensions={1}, use_global_device_ids=true | all-gather | bytes 491520 | tf_op jit(solution)/shard_map/all_gather | solution.py:116
  38.3 1.2 %fusion.35 = (f32[1,16,256]{2,1,0:T(8,128)S(1)}, f32[1,16,256]{2,1,0:T(8,128)S(1)}) fusion(f32[16,16,256]{2,1,0:T(8,128)S(1)} %add_divide_fusion.3, f32[16,16,256]{2,1,0:T(8,128)S(1)} %get-tuple-element.29, f32[]{:T(128)} %bitcast, f32[]{:T(128)} %bitcast.1), kind=kLoop, calls=%fused_computation.142 | loop fusion | flops 16384 | bytes 98312 | tf_op jit(solution)/shard_map/sub | solution.py:126
  39.5 13.5 %all_gather.9 = f32[8,16,256]{2,1,0:T(8,128)S(1)} all-gather(f32[2,16,256]{2,1,0:T(8,128)S(1)} %pad_maximum_fusion.19), channel_id=1, replica_groups=mesh['gx'=4,'gy'=2,'gz'=4] {'gz'}, dimensions={0}, use_global_device_ids=true | all-gather | bytes 163840 | tf_op jit(solution)/shard_map/all_gather | solution.py:129
  53.8 2.9 %collective-permute-start.4 = (f32[16,1,256]{2,1,0:T(1,128)S(1)}, f32[16,1,256]{2,1,0:T(1,128)S(1)}, u32[]{:S(2)}, u32[]{:S(2)}) collective-permute-start(f32[16,1,256]{2,1,0:T(1,128)S(1)} %get-tuple-element.74), channel_id=1, source_target_pairs={{8,0},{16,8},{24,16},{9,1},{17,9},{25,17},{10,2},{18,10},{26,18},{... | collective-permute-start | bytes 49160 | tf_op jit(solution)/shard_map/ppermute | solution.py:20
  56.7 2.9 %collective-permute-start.5 = (f32[16,1,256]{2,1,0:T(1,128)S(1)}, f32[16,1,256]{2,1,0:T(1,128)S(1)}, u32[]{:S(2)}, u32[]{:S(2)}) collective-permute-start(f32[16,1,256]{2,1,0:T(1,128)S(1)} %get-tuple-element.73), channel_id=1, source_target_pairs={{0,8},{8,16},{16,24},{1,9},{9,17},{17,25},{2,10},{10,18},{18,26},{... | collective-permute-start | bytes 49160 | tf_op jit(solution)/shard_map/ppermute | solution.py:17
  59.7 3.6 %collective-permute-done.5 = f32[16,1,256]{2,1,0:T(1,128)S(1)} collective-permute-done((f32[16,1,256]{2,1,0:T(1,128)S(1)}, f32[16,1,256]{2,1,0:T(1,128)S(1)}, u32[]{:S(2)}, u32[]{:S(2)}) %collective-permute-start.5) | collective-permute-done | bytes 16416 | tf_op jit(solution)/shard_map/ppermute | solution.py:17
  63.4 1.3 %collective-permute-start.6 = (f32[16,18,1]{2,1,0:T(8,128)S(1)}, f32[16,18,1]{2,1,0:T(8,128)S(1)}, u32[]{:S(2)}, u32[]{:S(2)}) collective-permute-start(f32[16,18,1]{2,1,0:T(8,128)S(1)} %get-tuple-element.55), channel_id=1, source_target_pairs={{4,0},{5,1},{6,2},{7,3},{12,8},{13,9},{14,10},{15,11},{20,16},{21,... | collective-permute-start | bytes 3464 | tf_op jit(solution)/shard_map/ppermute | solution.py:20
  64.7 3.0 %collective-permute-start.7 = (f32[16,18,1]{2,1,0:T(8,128)S(1)}, f32[16,18,1]{2,1,0:T(8,128)S(1)}, u32[]{:S(2)}, u32[]{:S(2)}) collective-permute-start(f32[16,18,1]{2,1,0:T(8,128)S(1)} %get-tuple-element.56), channel_id=1, source_target_pairs={{0,4},{1,5},{2,6},{3,7},{8,12},{9,13},{10,14},{11,15},{16,20},{17,... | collective-permute-start | bytes 3464 | tf_op jit(solution)/shard_map/ppermute | solution.py:17
  67.8 1.0 %collective-permute-done.7 = f32[16,18,1]{2,1,0:T(8,128)S(1)} collective-permute-done((f32[16,18,1]{2,1,0:T(8,128)S(1)}, f32[16,18,1]{2,1,0:T(8,128)S(1)}, u32[]{:S(2)}, u32[]{:S(2)}) %collective-permute-start.7) | collective-permute-done | bytes 1184 | tf_op jit(solution)/shard_map/ppermute | solution.py:17
  70.0 1.2 %fusion.31 = (f32[1,16,256]{2,1,0:T(8,128)S(1)}, f32[1,16,256]{2,1,0:T(8,128)S(1)}) fusion(f32[16,16,256]{2,1,0:T(8,128)S(1)} %add_divide_fusion, f32[16,16,256]{2,1,0:T(8,128)S(1)} %get-tuple-element.6, f32[]{:T(128)} %bitcast, f32[]{:T(128)} %bitcast.1), kind=kLoop, calls=%fused_computation.130 | loop fusion | flops 16384 | bytes 98312 | tf_op jit(solution)/shard_map/sub | solution.py:126
  71.2 13.4 %all_gather.11 = f32[8,16,256]{2,1,0:T(8,128)S(1)} all-gather(f32[2,16,256]{2,1,0:T(8,128)S(1)} %pad_maximum_fusion.20), channel_id=1, replica_groups=mesh['gx'=4,'gy'=2,'gz'=4] {'gz'}, dimensions={0}, use_global_device_ids=true | all-gather | bytes 163840 | tf_op jit(solution)/shard_map/all_gather | solution.py:129
  84.9 0.8 select_select_fusion
  (106 shorter events, 6.9 us)
Async XLA Ops:
  1.0 8.5 %collective-permute-start = (f32[16,1,256]{2,1,0:T(1,128)S(1)}, f32[16,1,256]{2,1,0:T(1,128)S(1)}, u32[]{:S(2)}, u32[]{:S(2)}) collective-permute-start(f32[16,1,256]{2,1,0:T(1,128)S(1)} %get-tuple-element.94), channel_id=1, source_target_pairs={{8,0},{16,8},{24,16},{9,1},{17,9},{25,17},{10,2},{18,10},{26,18},{... | collective-permute-start | bytes 49160 | tf_op jit(solution)/shard_map/ppermute | solution.py:20
  4.3 6.5 %collective-permute-start.1 = (f32[16,1,256]{2,1,0:T(1,128)S(1)}, f32[16,1,256]{2,1,0:T(1,128)S(1)}, u32[]{:S(2)}, u32[]{:S(2)}) collective-permute-start(f32[16,1,256]{2,1,0:T(1,128)S(1)} %get-tuple-element.93), channel_id=1, source_target_pairs={{0,8},{8,16},{16,24},{1,9},{9,17},{17,25},{2,10},{10,18},{18,26},{... | collective-permute-start | bytes 49160 | tf_op jit(solution)/shard_map/ppermute | solution.py:17
  6.9 0.7 copy-start.4
  8.2 1.3 %copy-start.3 = (s32[16,256]{1,0:T(8,128)S(1)}, s32[16,256]{1,0:T(8,128)}, u32[]{:S(2)}) copy-start(s32[16,256]{1,0:T(8,128)} %param.9) | copy-start | bytes 49156
  8.2 2.7 %copy-start = (f32[16,16,256]{2,1,0:T(8,128)S(1)}, f32[16,16,256]{2,1,0:T(8,128)}, u32[]{:S(2)}) copy-start(f32[16,16,256]{2,1,0:T(8,128)} %param.5) | copy-start | bytes 786436
  10.9 5.7 %copy-start.1 = (f32[16,16,256]{2,1,0:T(8,128)S(1)}, f32[16,16,256]{2,1,0:T(8,128)}, u32[]{:S(2)}) copy-start(f32[16,16,256]{2,1,0:T(8,128)} %param.6) | copy-start | bytes 786436
  11.0 5.7 %copy-start.2 = (f32[16,16,256]{2,1,0:T(8,128)S(1)}, f32[16,16,256]{2,1,0:T(8,128)}, u32[]{:S(2)}) copy-start(f32[16,16,256]{2,1,0:T(8,128)} %param.7) | copy-start | bytes 786436
  11.1 4.6 %collective-permute-start.2 = (f32[16,18,1]{2,1,0:T(8,128)S(1)}, f32[16,18,1]{2,1,0:T(8,128)S(1)}, u32[]{:S(2)}, u32[]{:S(2)}) collective-permute-start(f32[16,18,1]{2,1,0:T(8,128)S(1)} %get-tuple-element.63), channel_id=1, source_target_pairs={{4,0},{5,1},{6,2},{7,3},{12,8},{13,9},{14,10},{15,11},{20,16},{21,... | collective-permute-start | bytes 3464 | tf_op jit(solution)/shard_map/ppermute | solution.py:20
  12.5 4.1 %collective-permute-start.3 = (f32[16,18,1]{2,1,0:T(8,128)S(1)}, f32[16,18,1]{2,1,0:T(8,128)S(1)}, u32[]{:S(2)}, u32[]{:S(2)}) collective-permute-start(f32[16,18,1]{2,1,0:T(8,128)S(1)} %get-tuple-element.64), channel_id=1, source_target_pairs={{0,4},{1,5},{2,6},{3,7},{8,12},{9,13},{10,14},{11,15},{16,20},{17,... | collective-permute-start | bytes 3464 | tf_op jit(solution)/shard_map/ppermute | solution.py:17
  53.8 5.9 %collective-permute-start.4 = (f32[16,1,256]{2,1,0:T(1,128)S(1)}, f32[16,1,256]{2,1,0:T(1,128)S(1)}, u32[]{:S(2)}, u32[]{:S(2)}) collective-permute-start(f32[16,1,256]{2,1,0:T(1,128)S(1)} %get-tuple-element.74), channel_id=1, source_target_pairs={{8,0},{16,8},{24,16},{9,1},{17,9},{25,17},{10,2},{18,10},{26,18},{... | collective-permute-start | bytes 49160 | tf_op jit(solution)/shard_map/ppermute | solution.py:20
  56.7 6.5 %collective-permute-start.5 = (f32[16,1,256]{2,1,0:T(1,128)S(1)}, f32[16,1,256]{2,1,0:T(1,128)S(1)}, u32[]{:S(2)}, u32[]{:S(2)}) collective-permute-start(f32[16,1,256]{2,1,0:T(1,128)S(1)} %get-tuple-element.73), channel_id=1, source_target_pairs={{0,8},{8,16},{16,24},{1,9},{9,17},{17,25},{2,10},{10,18},{18,26},{... | collective-permute-start | bytes 49160 | tf_op jit(solution)/shard_map/ppermute | solution.py:17
  63.4 4.4 %collective-permute-start.6 = (f32[16,18,1]{2,1,0:T(8,128)S(1)}, f32[16,18,1]{2,1,0:T(8,128)S(1)}, u32[]{:S(2)}, u32[]{:S(2)}) collective-permute-start(f32[16,18,1]{2,1,0:T(8,128)S(1)} %get-tuple-element.55), channel_id=1, source_target_pairs={{4,0},{5,1},{6,2},{7,3},{12,8},{13,9},{14,10},{15,11},{20,16},{21,... | collective-permute-start | bytes 3464 | tf_op jit(solution)/shard_map/ppermute | solution.py:20
  64.7 4.1 %collective-permute-start.7 = (f32[16,18,1]{2,1,0:T(8,128)S(1)}, f32[16,18,1]{2,1,0:T(8,128)S(1)}, u32[]{:S(2)}, u32[]{:S(2)}) collective-permute-start(f32[16,18,1]{2,1,0:T(8,128)S(1)} %get-tuple-element.56), channel_id=1, source_target_pairs={{0,4},{1,5},{2,6},{3,7},{8,12},{9,13},{10,14},{11,15},{16,20},{17,... | collective-permute-start | bytes 3464 | tf_op jit(solution)/shard_map/ppermute | solution.py:17
where the time goes:
time: 86.1 us; the launch traced here: 85.7 us
  blocking collectives  42.6 us (49%)
  starting transfers between devices  20.5 us (24%)
  other arithmetic  9.26 us (11%)
  waiting for transfers between devices  6.93 us (8%)
  local copies, waits for them, and re-layouts  5.68 us (7%)
    all_gather x2, blocking collectives, on_device(): all_sources = lax.all_gather(source_pair, 'gz', axis=0, tiled=True)  26.9 us
    all_gather x1, blocking collectives, on_device(): gathered = lax.all_gather(coupled, 'gz', axis=1, tiled=True)  15.6 us
    ppermute x4, starting transfers between devices, extended(): lax.ppermute(lax.slice_in_dim(block, block.shape[dim] - width, None, axis...  11.5 us
    ppermute x4, starting transfers between devices, extended(): lax.ppermute(lax.slice_in_dim(block, 0, width, axis=dim), axis, backward)  8.96 us
    ppermute x4, waiting for transfers between devices, extended(): lax.ppermute(lax.slice_in_dim(block, block.shape[dim] - width, None, axis...  6.92 us
    sub x2, other arithmetic, on_device(): first_source = source[0] - high_full[0] * interior[1]  2.43 us
    add x10, other arithmetic, apply_local(): source + weight_low * move_rows(source, stride, 0.0)  1.9 us
  transfers between devices with their start and end apart: 8, of which 4 were waited for; matrix products, arithmetic and copies ran while one was open for 2% of the time, Pallas kernels for 0%

commit v1 on v0

--- a/solution.py
+++ b/solution.py
@@ -113,7 +113,14 @@
         ],
         0,
     )
-    gathered = lax.all_gather(coupled, "gz", axis=1, tiled=True)
+    peers = lax.axis_size("gz")
+    right = [(i_2, (i_2 + 1) % peers) for i_2 in range(peers)]
+    parts = [coupled]
+    for far in range(1, peers):
+        parts = [lax.ppermute(parts[0], "gz", right), *parts]
+    full = jnp.concatenate(parts, axis=1)
+    turn = (lax.axis_index("gz") + 1) * parts[-1].shape[1]
+    gathered = jnp.roll(full, turn, axis=1)
     sections_reduced, centre_reduced = factor_local(gathered[0], gathered[1], gathered[2])
     iterate = correction
     for colour in range(2):

time: 86.1 us -> 81.9 us (0.951)
  the two profiles are of different devices: /device:TPU:12 before, /device:TPU:4 now
where the time goes in v1:
time: 81.9 us; the launch traced here: 81.6 us
  blocking collectives  27.1 us (33%)
  starting transfers between devices  22.3 us (27%)
  waiting for transfers between devices  16.3 us (20%)
  other arithmetic  9.31 us (11%)
  local copies, waits for them, and re-layouts  5.63 us (7%)
  between operations  0.82 us (1%)
    all_gather x2, blocking collectives, on_device(): all_sources = lax.all_gather(source_pair, 'gz', axis=0, tiled=True)  27.1 us
    ppermute x4, starting transfers between devices, extended(): lax.ppermute(lax.slice_in_dim(block, block.shape[dim] - width, None, axis...  9.8 us
    ppermute x4, starting transfers between devices, extended(): lax.ppermute(lax.slice_in_dim(block, 0, width, axis=dim), axis, backward)  8.95 us
    ppermute x3, waiting for transfers between devices, on_device(): parts = [lax.ppermute(parts[0], 'gz', right), *parts]  8.35 us
    ppermute x4, waiting for transfers between devices, extended(): lax.ppermute(lax.slice_in_dim(block, block.shape[dim] - width, None, axis...  5.95 us
    ppermute x3, starting transfers between devices, on_device(): parts = [lax.ppermute(parts[0], 'gz', right), *parts]  3.58 us
    sub x2, other arithmetic, on_device(): first_source = source[0] - high_full[0] * interior[1]  2.45 us
    ppermute x4, waiting for transfers between devices, extended(): lax.ppermute(lax.slice_in_dim(block, 0, width, axis=dim), axis, backward)  2.03 us
  transfers between devices with their start and end apart: 11, of which 6 were waited for; matrix products, arithmetic and copies ran while one was open for 4% of the time, Pallas kernels for 0%

profile of v1, /device:TPU:4, one launch (start us, length us, event | category | flops | bytes accessed | tf_op | source)
XLA Modules:
  0.0 81.6 jit_solution(6691374906991897618)
XLA Ops:
  0.0 1.0 %fusion.55 = (f32[16,1,256]{2,1,0:T(1,128)S(1)}, f32[16,1,256]{2,1,0:T(1,128)S(1)}) fusion(f32[16,16,256]{2,1,0:T(8,128)} %param.5), kind=kLoop, calls=%fused_computation.178 | loop fusion | bytes 65536 | tf_op jit(solution)/shard_map/slice | solution.py:18
  1.0 3.3 %collective-permute-start = (f32[16,1,256]{2,1,0:T(1,128)S(1)}, f32[16,1,256]{2,1,0:T(1,128)S(1)}, u32[]{:S(2)}, u32[]{:S(2)}) collective-permute-start(f32[16,1,256]{2,1,0:T(1,128)S(1)} %get-tuple-element.94), channel_id=1, source_target_pairs={{8,0},{16,8},{24,16},{9,1},{17,9},{25,17},{10,2},{18,10},{26,18},{... | collective-permute-start | bytes 49160 | tf_op jit(solution)/shard_map/ppermute | solution.py:20
  4.3 2.5 %collective-permute-start.1 = (f32[16,1,256]{2,1,0:T(1,128)S(1)}, f32[16,1,256]{2,1,0:T(1,128)S(1)}, u32[]{:S(2)}, u32[]{:S(2)}) collective-permute-start(f32[16,1,256]{2,1,0:T(1,128)S(1)} %get-tuple-element.93), channel_id=1, source_target_pairs={{0,8},{8,16},{16,24},{1,9},{9,17},{17,25},{2,10},{10,18},{18,26},{... | collective-permute-start | bytes 49160 | tf_op jit(solution)/shard_map/ppermute | solution.py:17
  9.5 1.4 %collective-permute-done.1 = f32[16,1,256]{2,1,0:T(1,128)S(1)} collective-permute-done((f32[16,1,256]{2,1,0:T(1,128)S(1)}, f32[16,1,256]{2,1,0:T(1,128)S(1)}, u32[]{:S(2)}, u32[]{:S(2)}) %collective-permute-start.1) | collective-permute-done | bytes 16416 | tf_op jit(solution)/shard_map/ppermute | solution.py:17
  11.1 1.4 %collective-permute-start.2 = (f32[16,18,1]{2,1,0:T(8,128)S(1)}, f32[16,18,1]{2,1,0:T(8,128)S(1)}, u32[]{:S(2)}, u32[]{:S(2)}) collective-permute-start(f32[16,18,1]{2,1,0:T(8,128)S(1)} %get-tuple-element.63), channel_id=1, source_target_pairs={{4,0},{5,1},{6,2},{7,3},{12,8},{13,9},{14,10},{15,11},{20,16},{21,... | collective-permute-start | bytes 3464 | tf_op jit(solution)/shard_map/ppermute | solution.py:20
  12.5 3.0 %collective-permute-start.3 = (f32[16,18,1]{2,1,0:T(8,128)S(1)}, f32[16,18,1]{2,1,0:T(8,128)S(1)}, u32[]{:S(2)}, u32[]{:S(2)}) collective-permute-start(f32[16,18,1]{2,1,0:T(8,128)S(1)} %get-tuple-element.64), channel_id=1, source_target_pairs={{0,4},{1,5},{2,6},{3,7},{8,12},{9,13},{10,14},{11,15},{16,20},{17,... | collective-permute-start | bytes 3464 | tf_op jit(solution)/shard_map/ppermute | solution.py:17
  15.6 1.0 %collective-permute-done.3 = f32[16,18,1]{2,1,0:T(8,128)S(1)} collective-permute-done((f32[16,18,1]{2,1,0:T(8,128)S(1)}, f32[16,18,1]{2,1,0:T(8,128)S(1)}, u32[]{:S(2)}, u32[]{:S(2)}) %collective-permute-start.3) | collective-permute-done | bytes 1184 | tf_op jit(solution)/shard_map/ppermute | solution.py:17
  19.8 1.2 %slice_multiply_fusion.5 = (f32[1,16,256]{2,1,0:T(8,128)S(1)}, f32[1,16,256]{2,1,0:T(8,128)S(1)}, f32[1,16,256]{2,1,0:T(8,128)S(1)}, f32[1,16,256]{2,1,0:T(8,128)S(1)}) fusion(f32[16,16,256]{2,1,0:T(8,128)S(1)} %get-tuple-element.36, f32[]{:T(128)} %bitcast.1, f32[]{:T(128)} %bitcast, f32[16,16,256]{2,1,0:T(8,128)S(1)} %get-tuple-element.158, ...), kind=kLoop, calls=%fused_computation.146 | loop fusion | flops 24576 | bytes 163848 | tf_op jit(solution)/shard_map/mul | solution.py:105
  21.0 0.7 pad_bitcast_fusion.1
  22.4 1.6 %collective-permute-start.4 = (f32[3,2,16,256]{3,2,1,0:T(8,128)S(1)}, f32[3,2,16,256]{3,2,1,0:T(8,128)S(1)}, u32[]{:S(2)}, u32[]{:S(2)}) collective-permute-start(f32[3,2,16,256]{3,2,1,0:T(8,128)S(1)} %pad_maximum_fusion.18), channel_id=1, source_target_pairs={{0,1},{1,2},{2,3},{3,0},{4,5},{5,6},{6,7},{7,4},{8,9},{9,10},{10,1... | collective-permute-start | bytes 294920 | tf_op jit(solution)/shard_map/ppermute | solution.py:120
  24.2 1.2 %fusion.35 = (f32[1,16,256]{2,1,0:T(8,128)S(1)}, f32[1,16,256]{2,1,0:T(8,128)S(1)}) fusion(f32[16,16,256]{2,1,0:T(8,128)S(1)} %add_divide_fusion.3, f32[16,16,256]{2,1,0:T(8,128)S(1)} %get-tuple-element.29, f32[]{:T(128)} %bitcast, f32[]{:T(128)} %bitcast.1), kind=kLoop, calls=%fused_computation.150 | loop fusion | flops 16384 | bytes 98312 | tf_op jit(solution)/shard_map/sub | solution.py:133
  25.5 3.9 %collective-permute-done.4 = f32[3,2,16,256]{3,2,1,0:T(8,128)S(1)} collective-permute-done((f32[3,2,16,256]{3,2,1,0:T(8,128)S(1)}, f32[3,2,16,256]{3,2,1,0:T(8,128)S(1)}, u32[]{:S(2)}, u32[]{:S(2)}) %collective-permute-start.4) | collective-permute-done | bytes 98336 | tf_op jit(solution)/shard_map/ppermute | solution.py:120
  29.4 13.8 %all_gather.6 = f32[8,16,256]{2,1,0:T(8,128)S(1)} all-gather(f32[2,16,256]{2,1,0:T(8,128)S(1)} %pad_maximum_fusion.19), channel_id=1, replica_groups=mesh['gx'=4,'gy'=2,'gz'=4] {'gz'}, dimensions={0}, use_global_device_ids=true | all-gather | bytes 163840 | tf_op jit(solution)/shard_map/all_gather | solution.py:136
  43.2 1.9 %collective-permute-start.6 = (f32[3,2,16,256]{3,2,1,0:T(8,128)S(1)}, f32[3,2,16,256]{3,2,1,0:T(8,128)S(1)}, u32[]{:S(2)}, u32[]{:S(2)}) collective-permute-start(f32[3,2,16,256]{3,2,1,0:T(8,128)S(1)} %collective-permute-done.5), channel_id=1, source_target_pairs={{0,1},{1,2},{2,3},{3,0},{4,5},{5,6},{6,7},{7,4},{8,9},{9,10},{10,1... | collective-permute-start | bytes 294920 | tf_op jit(solution)/shard_map/ppermute | solution.py:120
  45.1 4.5 %collective-permute-done.6 = f32[3,2,16,256]{3,2,1,0:T(8,128)S(1)} collective-permute-done((f32[3,2,16,256]{3,2,1,0:T(8,128)S(1)}, f32[3,2,16,256]{3,2,1,0:T(8,128)S(1)}, u32[]{:S(2)}, u32[]{:S(2)}) %collective-permute-start.6) | collective-permute-done | bytes 98336 | tf_op jit(solution)/shard_map/ppermute | solution.py:120
  50.5 2.9 %collective-permute-start.7 = (f32[16,1,256]{2,1,0:T(1,128)S(1)}, f32[16,1,256]{2,1,0:T(1,128)S(1)}, u32[]{:S(2)}, u32[]{:S(2)}) collective-permute-start(f32[16,1,256]{2,1,0:T(1,128)S(1)} %get-tuple-element.74), channel_id=1, source_target_pairs={{8,0},{16,8},{24,16},{9,1},{17,9},{25,17},{10,2},{18,10},{26,18},{... | collective-permute-start | bytes 49160 | tf_op jit(solution)/shard_map/ppermute | solution.py:20
  53.4 2.9 %collective-permute-start.8 = (f32[16,1,256]{2,1,0:T(1,128)S(1)}, f32[16,1,256]{2,1,0:T(1,128)S(1)}, u32[]{:S(2)}, u32[]{:S(2)}) collective-permute-start(f32[16,1,256]{2,1,0:T(1,128)S(1)} %get-tuple-element.73), channel_id=1, source_target_pairs={{0,8},{8,16},{16,24},{1,9},{9,17},{17,25},{2,10},{10,18},{18,26},{... | collective-permute-start | bytes 49160 | tf_op jit(solution)/shard_map/ppermute | solution.py:17
  56.4 3.6 %collective-permute-done.8 = f32[16,1,256]{2,1,0:T(1,128)S(1)} collective-permute-done((f32[16,1,256]{2,1,0:T(1,128)S(1)}, f32[16,1,256]{2,1,0:T(1,128)S(1)}, u32[]{:S(2)}, u32[]{:S(2)}) %collective-permute-start.8) | collective-permute-done | bytes 16416 | tf_op jit(solution)/shard_map/ppermute | solution.py:17
  60.1 1.3 %collective-permute-start.10 = (f32[16,18,1]{2,1,0:T(8,128)S(1)}, f32[16,18,1]{2,1,0:T(8,128)S(1)}, u32[]{:S(2)}, u32[]{:S(2)}) collective-permute-start(f32[16,18,1]{2,1,0:T(8,128)S(1)} %get-tuple-element.62), channel_id=1, source_target_pairs={{0,4},{1,5},{2,6},{3,7},{8,12},{9,13},{10,14},{11,15},{16,20},{17,... | collective-permute-start | bytes 3464 | tf_op jit(solution)/shard_map/ppermute | solution.py:17
  61.5 1.3 %collective-permute-start.9 = (f32[16,18,1]{2,1,0:T(8,128)S(1)}, f32[16,18,1]{2,1,0:T(8,128)S(1)}, u32[]{:S(2)}, u32[]{:S(2)}) collective-permute-start(f32[16,18,1]{2,1,0:T(8,128)S(1)} %get-tuple-element.61), channel_id=1, source_target_pairs={{4,0},{5,1},{6,2},{7,3},{12,8},{13,9},{14,10},{15,11},{20,16},{21,... | collective-permute-start | bytes 3464 | tf_op jit(solution)/shard_map/ppermute | solution.py:20
  62.8 2.0 %collective-permute-done.9 = f32[16,18,1]{2,1,0:T(8,128)S(1)} collective-permute-done((f32[16,18,1]{2,1,0:T(8,128)S(1)}, f32[16,18,1]{2,1,0:T(8,128)S(1)}, u32[]{:S(2)}, u32[]{:S(2)}) %collective-permute-start.9) | collective-permute-done | bytes 1184 | tf_op jit(solution)/shard_map/ppermute | solution.py:20
  65.9 1.2 %fusion.31 = (f32[1,16,256]{2,1,0:T(8,128)S(1)}, f32[1,16,256]{2,1,0:T(8,128)S(1)}) fusion(f32[16,16,256]{2,1,0:T(8,128)S(1)} %add_divide_fusion, f32[16,16,256]{2,1,0:T(8,128)S(1)} %get-tuple-element.6, f32[]{:T(128)} %bitcast, f32[]{:T(128)} %bitcast.1), kind=kLoop, calls=%fused_computation.138 | loop fusion | flops 16384 | bytes 98312 | tf_op jit(solution)/shard_map/sub | solution.py:133
  67.2 13.3 %all_gather.7 = f32[8,16,256]{2,1,0:T(8,128)S(1)} all-gather(f32[2,16,256]{2,1,0:T(8,128)S(1)} %pad_maximum_fusion.20), channel_id=1, replica_groups=mesh['gx'=4,'gy'=2,'gz'=4] {'gz'}, dimensions={0}, use_global_device_ids=true | all-gather | bytes 163840 | tf_op jit(solution)/shard_map/all_gather | solution.py:136
  80.8 0.8 %select_select_fusion = f32[16,16,256]{2,1,0:T(8,128)} fusion(f32[16,16,256]{2,1,0:T(8,128)S(1)} %select_select_fusion.1, f32[16,16,256]{2,1,0:T(8,128)S(1)} %get-tuple-element.37, f32[16,16,256]{2,1,0:T(8,128)S(1)} %add_divide_fusion, f32[16,16,256]{2,1,0:T(8,128)S(1)} %get-tuple-element.36, f32[16,256]{1,0:T(8,128)S(1)} %get-tuple-element.152, ...), kind=kLoop, calls=%fused_computation.32 | loop fusion | flops 458752 | bytes 1347616 | tf_op jit(solution)/shard_map/jit(_where)/select_n | solution.py:147
  (119 shorter events, 8.8 us)
Async XLA Ops:
  1.0 8.5 %collective-permute-start = (f32[16,1,256]{2,1,0:T(1,128)S(1)}, f32[16,1,256]{2,1,0:T(1,128)S(1)}, u32[]{:S(2)}, u32[]{:S(2)}) collective-permute-start(f32[16,1,256]{2,1,0:T(1,128)S(1)} %get-tuple-element.94), channel_id=1, source_target_pairs={{8,0},{16,8},{24,16},{9,1},{17,9},{25,17},{10,2},{18,10},{26,18},{... | collective-permute-start | bytes 49160 | tf_op jit(solution)/shard_map/ppermute | solution.py:20
  4.3 6.5 %collective-permute-start.1 = (f32[16,1,256]{2,1,0:T(1,128)S(1)}, f32[16,1,256]{2,1,0:T(1,128)S(1)}, u32[]{:S(2)}, u32[]{:S(2)}) collective-permute-start(f32[16,1,256]{2,1,0:T(1,128)S(1)} %get-tuple-element.93), channel_id=1, source_target_pairs={{0,8},{8,16},{16,24},{1,9},{9,17},{17,25},{2,10},{10,18},{18,26},{... | collective-permute-start | bytes 49160 | tf_op jit(solution)/shard_map/ppermute | solution.py:17
  6.9 0.7 copy-start.4
  8.2 1.2 %copy-start.3 = (s32[16,256]{1,0:T(8,128)S(1)}, s32[16,256]{1,0:T(8,128)}, u32[]{:S(2)}) copy-start(s32[16,256]{1,0:T(8,128)} %param.9) | copy-start | bytes 49156
  8.2 2.7 %copy-start = (f32[16,16,256]{2,1,0:T(8,128)S(1)}, f32[16,16,256]{2,1,0:T(8,128)}, u32[]{:S(2)}) copy-start(f32[16,16,256]{2,1,0:T(8,128)} %param.5) | copy-start | bytes 786436
  10.9 5.7 %copy-start.1 = (f32[16,16,256]{2,1,0:T(8,128)S(1)}, f32[16,16,256]{2,1,0:T(8,128)}, u32[]{:S(2)}) copy-start(f32[16,16,256]{2,1,0:T(8,128)} %param.6) | copy-start | bytes 786436
  11.0 5.7 %copy-start.2 = (f32[16,16,256]{2,1,0:T(8,128)S(1)}, f32[16,16,256]{2,1,0:T(8,128)}, u32[]{:S(2)}) copy-start(f32[16,16,256]{2,1,0:T(8,128)} %param.7) | copy-start | bytes 786436
  11.1 4.5 %collective-permute-start.2 = (f32[16,18,1]{2,1,0:T(8,128)S(1)}, f32[16,18,1]{2,1,0:T(8,128)S(1)}, u32[]{:S(2)}, u32[]{:S(2)}) collective-permute-start(f32[16,18,1]{2,1,0:T(8,128)S(1)} %get-tuple-element.63), channel_id=1, source_target_pairs={{4,0},{5,1},{6,2},{7,3},{12,8},{13,9},{14,10},{15,11},{20,16},{21,... | collective-permute-start | bytes 3464 | tf_op jit(solution)/shard_map/ppermute | solution.py:20
  12.5 4.1 %collective-permute-start.3 = (f32[16,18,1]{2,1,0:T(8,128)S(1)}, f32[16,18,1]{2,1,0:T(8,128)S(1)}, u32[]{:S(2)}, u32[]{:S(2)}) collective-permute-start(f32[16,18,1]{2,1,0:T(8,128)S(1)} %get-tuple-element.64), channel_id=1, source_target_pairs={{0,4},{1,5},{2,6},{3,7},{8,12},{9,13},{10,14},{11,15},{16,20},{17,... | collective-permute-start | bytes 3464 | tf_op jit(solution)/shard_map/ppermute | solution.py:17
  22.4 7.0 %collective-permute-start.4 = (f32[3,2,16,256]{3,2,1,0:T(8,128)S(1)}, f32[3,2,16,256]{3,2,1,0:T(8,128)S(1)}, u32[]{:S(2)}, u32[]{:S(2)}) collective-permute-start(f32[3,2,16,256]{3,2,1,0:T(8,128)S(1)} %pad_maximum_fusion.18), channel_id=1, source_target_pairs={{0,1},{1,2},{2,3},{3,0},{4,5},{5,6},{6,7},{7,4},{8,9},{9,10},{10,1... | collective-permute-start | bytes 294920 | tf_op jit(solution)/shard_map/ppermute | solution.py:120
  29.3 13.8 %collective-permute-start.5 = (f32[3,2,16,256]{3,2,1,0:T(8,128)S(1)}, f32[3,2,16,256]{3,2,1,0:T(8,128)S(1)}, u32[]{:S(2)}, u32[]{:S(2)}) collective-permute-start(f32[3,2,16,256]{3,2,1,0:T(8,128)S(1)} %collective-permute-done.4), channel_id=1, source_target_pairs={{0,1},{1,2},{2,3},{3,0},{4,5},{5,6},{6,7},{7,4},{8,9},{9,10},{10,1... | collective-permute-start | bytes 294920 | tf_op jit(solution)/shard_map/ppermute | solution.py:120
  43.2 6.4 %collective-permute-start.6 = (f32[3,2,16,256]{3,2,1,0:T(8,128)S(1)}, f32[3,2,16,256]{3,2,1,0:T(8,128)S(1)}, u32[]{:S(2)}, u32[]{:S(2)}) collective-permute-start(f32[3,2,16,256]{3,2,1,0:T(8,128)S(1)} %collective-permute-done.5), channel_id=1, source_target_pairs={{0,1},{1,2},{2,3},{3,0},{4,5},{5,6},{6,7},{7,4},{8,9},{9,10},{10,1... | collective-permute-start | bytes 294920 | tf_op jit(solution)/shard_map/ppermute | solution.py:120
  50.5 5.9 %collective-permute-start.7 = (f32[16,1,256]{2,1,0:T(1,128)S(1)}, f32[16,1,256]{2,1,0:T(1,128)S(1)}, u32[]{:S(2)}, u32[]{:S(2)}) collective-permute-start(f32[16,1,256]{2,1,0:T(1,128)S(1)} %get-tuple-element.74), channel_id=1, source_target_pairs={{8,0},{16,8},{24,16},{9,1},{17,9},{25,17},{10,2},{18,10},{26,18},{... | collective-permute-start | bytes 49160 | tf_op jit(solution)/shard_map/ppermute | solution.py:20
  53.4 6.5 %collective-permute-start.8 = (f32[16,1,256]{2,1,0:T(1,128)S(1)}, f32[16,1,256]{2,1,0:T(1,128)S(1)}, u32[]{:S(2)}, u32[]{:S(2)}) collective-permute-start(f32[16,1,256]{2,1,0:T(1,128)S(1)} %get-tuple-element.73), channel_id=1, source_target_pairs={{0,8},{8,16},{16,24},{1,9},{9,17},{17,25},{2,10},{10,18},{18,26},{... | collective-permute-start | bytes 49160 | tf_op jit(solution)/shard_map/ppermute | solution.py:17
  60.1 2.6 %collective-permute-start.10 = (f32[16,18,1]{2,1,0:T(8,128)S(1)}, f32[16,18,1]{2,1,0:T(8,128)S(1)}, u32[]{:S(2)}, u32[]{:S(2)}) collective-permute-start(f32[16,18,1]{2,1,0:T(8,128)S(1)} %get-tuple-element.62), channel_id=1, source_target_pairs={{0,4},{1,5},{2,6},{3,7},{8,12},{9,13},{10,14},{11,15},{16,20},{17,... | collective-permute-start | bytes 3464 | tf_op jit(solution)/shard_map/ppermute | solution.py:17
  61.5 3.3 %collective-permute-start.9 = (f32[16,18,1]{2,1,0:T(8,128)S(1)}, f32[16,18,1]{2,1,0:T(8,128)S(1)}, u32[]{:S(2)}, u32[]{:S(2)}) collective-permute-start(f32[16,18,1]{2,1,0:T(8,128)S(1)} %get-tuple-element.61), channel_id=1, source_target_pairs={{4,0},{5,1},{6,2},{7,3},{12,8},{13,9},{14,10},{15,11},{20,16},{21,... | collective-permute-start | bytes 3464 | tf_op jit(solution)/shard_map/ppermute | solution.py:20
